TPU v7x, 32 devices: a whole 2x2x4 slice. The times are simulated.
32 devices in a mesh: cls: 4 (over x, core), prt: 8 (over z, y).
Axes of the slice: x: 2, y: 2, z: 4, core: 2. Of those that a mesh axis runs over, the one named last changes fastest.
Arguments:
- images: bfloat16 [4096, 7168], P(('cls', 'prt')), may hold values from -48 to 48
- projections: bfloat16 [8, 144, 7168], P('cls', None, 'prt'), may hold values from -5 to 5
- noise_weights: float32 [7168], replicated, may hold values from 0.005 to 0.03
- class_prior: float32 [8], replicated, may hold values from 0.05 to 1
- class_lists: int32 [4096, 2], P(('cls', 'prt')), may hold values from 0 to 7, all different within a row; in each aligned block of 128 rows (0 to 127, 128 to 255, ...) at most 40 rows name the same one
Outputs:
- class_sums: float32 [8, 144, 7168], P('cls', None, 'prt')
- class_weights: float32 [8, 144], P('cls')
- evidence: float32 [4096], P(('cls', 'prt'))
Inputs may be any that keep to these rules, and one draw needn't show every extreme that they name: `class_lists`: each row names 2 different classes; in the rows of one device no class is named by more than 40 rows, a bound that some block reaches.
All inputs are finite; a program needn't handle non-finite values.
Results may differ from a plain program's by a relative error of at most 0.0066.
Values may be sent and summed in bfloat16 or wider, within the bound.
No kernel may reach another device: no remote copies, remote signals or barrier semaphores. Data moves between devices by JAX's collectives and lax.ppermute only.
A program may use at most 128 MiB of HBM per device.

v0:
```python
import jax
import jax.numpy as jnp
from jax import lax
from jax.sharding import PartitionSpec as P


def score_columns(slab, weighted, noise_weights):
    count = slab.shape[0]
    orient = slab.shape[1]
    nrows = weighted.shape[0]
    piece = lax.all_gather(slab, "prt", axis=2, tiled=True)
    span = piece.shape[2]
    flat = piece.reshape(count * orient, span)
    cross = lax.dot_general(
        weighted, flat, (((1,), (1,)), ((), ())), preferred_element_type=jnp.float32
    )
    square = piece.astype(jnp.float32)
    norms = 0.5 * jnp.sum(square * square * noise_weights[None, None, :], axis=2).reshape(
        count * orient
    )
    cross, norms = (cross, norms)
    return (cross - norms[None, :]).reshape(nrows, count, orient)


def posterior(score, log_prior, listed):
    score = score + log_prior[None, :, None]
    score = jnp.where(listed[:, :, None], score, -jnp.inf)
    top = jnp.max(score, axis=(1, 2))
    total = jnp.sum(jnp.exp(score - top[:, None, None]), axis=(1, 2))
    evid = top + jnp.log(total)
    post = jnp.exp(score - evid[:, None, None]).astype(jnp.bfloat16)
    return (evid, post)


def local(images, projections, noise_weights, class_prior, class_lists):
    groups = lax.axis_size("cls")
    owned = projections.shape[0]
    classes = owned * groups
    log_prior = jnp.log(class_prior)
    listed = jnp.any(
        class_lists[:, :, None] == jnp.arange(classes, dtype=jnp.int32)[None, None, :], axis=1
    )
    everyone = lax.all_gather(images, "cls", axis=0, tiled=True)
    weighted = (everyone.astype(jnp.float32) * noise_weights[None, :]).astype(jnp.bfloat16)
    own_scores = score_columns(projections, weighted, noise_weights)
    score = lax.all_to_all(own_scores, "cls", split_axis=0, concat_axis=1, tiled=True)
    evidence, post = posterior(score, log_prior, listed)
    mine = lax.all_to_all(post, "cls", split_axis=1, concat_axis=0, tiled=True)
    sums = jnp.einsum("ijr,if->jrf", mine, everyone, preferred_element_type=jnp.float32)
    totals = jnp.sum(mine.astype(jnp.float32), axis=0)
    class_sums = lax.psum_scatter(sums, "prt", scatter_dimension=2, tiled=True)
    class_weights = lax.psum(totals, "prt")
    return (class_sums, class_weights, evidence)


def solution(mesh):
    return jax.shard_map(
        local,
        mesh=mesh,
        in_specs=(
            P(("cls", "prt"), None),
            P("cls", None, "prt"),
            P(),
            P(),
            P(("cls", "prt"), None),
        ),
        out_specs=(P("cls", None, "prt"), P("cls", None), P(("cls", "prt"))),
        check_vma=False,
    )
```

profile of v0, /device:TPU:0, one launch (start us, length us, event | category | flops | bytes accessed | tf_op | source)
XLA Modules:
  0.0 335.4 jit_solution(646722921677598677)
XLA Ops:
  7.2 0.0 all-gather.5.cloned.1.call-start
  7.2 0.7 all-gather.5.cloned.1.call-update
  7.9 0.0 all-gather.3.cloned.1.call-start
  7.9 0.7 all-gather.3.cloned.1.call-update
  8.6 76.2 %all-gather.5.cloned.1.call-done = bf16[2,144,7168]{2,1,0:T(8,128)(2,1)} async-done(((bf16[2,144,896]{2,1,0:T(8,128)(2,1)}), bf16[2,144,7168]{2,1,0:T(8,128)(2,1)}) %all-gather.5.cloned.1.call-update) | async-done | bytes 4128784 | tf_op jit(solution)/shard_map/all_gather | solution.py:11
  84.9 3.3 multiply_reduce_fusion
  88.2 0.1 mul.39
  88.3 49.0 %all-gather.3.cloned.1.call-done = bf16[512,7168]{1,0:T(8,128)(2,1)} async-done(((bf16[128,7168]{1,0:T(8,128)(2,1)}), bf16[512,7168]{1,0:T(8,128)(2,1)}) %all-gather.3.cloned.1.call-update) | async-done | bytes 7340048 | tf_op jit(solution)/shard_map/all_gather | solution.py:43
  137.3 6.6 %fusion.4 = f32[512,288]{0,1:T(8,128)S(1)} fusion(bf16[288,7168]{1,0:T(8,128)(2,1)} %bitcast.31, bf16[512,7168]{1,0:T(8,128)(2,1)} %all-gather.3.cloned.1.call-done, f32[7168]{0:T(1024)} %param.7, f32[288]{0:T(512)S(1)} %mul.39), kind=kOutput, calls=%fused_computation.6 | convolution fusion | flops 2125086720 | bytes 12088448 | tf_op jit(solution)/shard_map/dot_general | solution.py:14
  143.9 1.3 copy.24
  145.2 3.5 %all-to-all-start = ((f32[512,2,144]{2,1,0:T(2,128)}), f32[512,2,144]{2,1,0:T(2,128)S(1)}, u32[]{:S(2)}, u32[]{:S(2)}) async-start(f32[512,2,144]{2,1,0:T(2,128)} %copy.24), calls=%async_computation | async-start | bytes 2097152 | tf_op jit(solution)/shard_map/all_to_all | solution.py:46
  148.8 0.0 reduce-scatter.2.cloned.1.call-start
  148.9 0.1 add.29
  149.0 0.1 copy.28
  149.1 14.1 %all-to-all-done = f32[512,2,144]{2,1,0:T(2,128)S(1)} async-done(((f32[512,2,144]{2,1,0:T(2,128)}), f32[512,2,144]{2,1,0:T(2,128)S(1)}, u32[]{:S(2)}, u32[]{:S(2)}) %all-to-all-start) | async-done | bytes 589856 | tf_op jit(solution)/shard_map/all_to_all | solution.py:46
  163.2 1.0 copy.30
  164.2 0.4 fusion.9
  164.6 0.4 exponential_reduce_fusion
  165.0 0.2 fusion.8
  165.2 8.7 %all_to_all.36 = bf16[128,8,144]{0,2,1:T(8,128)(2,1)S(1)} all-to-all(bf16[128,8,144]{0,2,1:T(8,128)(2,1)S(1)} %fusion.8), channel_id=1, replica_groups=mesh['cls'=4,'prt'=8] {'cls'}, dimensions={1} | all-to-all | bytes 589824 | tf_op jit(solution)/shard_map/all_to_all | solution.py:48
  173.9 8.6 %fusion.1 = f32[2,144,7168]{2,1,0:T(8,128)} fusion(bf16[512,7168]{1,0:T(8,128)(2,1)} %all-gather.3.cloned.1.call-done, bf16[4,2,18,8,128]{4,3,2,1,0:T(8,128)(2,1)S(1)} %bitcast.32), kind=kOutput, calls=%fused_computation.3 | convolution fusion | flops 2113929216 | bytes 15892480 | tf_op jit(solution)/shard_map/ijr,if->jrf/dot_general | solution.py:49
  182.5 0.2 convert_reduce_fusion
  182.7 22.6 %psum.7 = f32[2,144]{1,0:T(2,128)} all-reduce(f32[2,144]{1,0:T(2,128)S(1)} %convert_reduce_fusion), channel_id=1, replica_groups=mesh['cls'=4,'prt'=8] {'prt'}, use_global_device_ids=true, to_apply=%region_6.7 | all-reduce | flops 288 | bytes 2304 | tf_op jit(solution)/shard_map/psum | solution.py:52
  205.3 123.5 %reduce-scatter.2.cloned.1.call-done = f32[2,144,896]{2,1,0:T(8,128)} async-done(((f32[2,144,7168]{2,1,0:T(8,128)}), f32[2,144,896]{2,1,0:T(8,128)}) %reduce-scatter.2.cloned.1.call-update) | async-done | bytes 1032208 | tf_op jit(solution)/shard_map/reduce_scatter | solution.py:51
  (14 shorter events, 0.1 us)
Async XLA Ops:
  7.2 77.7 %all-gather.5.cloned.1.call-start = ((), (), s32[]{:S(2)}) async-start(), calls=%async_computation.4 | async-start | bytes 4644864 | tf_op jit(solution)/shard_map/all_gather | solution.py:11
  7.9 129.4 %all-gather.3.cloned.1.call-start = ((), (), s32[]{:S(2)}) async-start(), calls=%async_computation.3 | async-start | bytes 9175040 | tf_op jit(solution)/shard_map/all_gather | solution.py:43
  137.3 11.5 %copy-start = (s32[128,2]{0,1:T(2,128)S(1)}, s32[128,2]{0,1:T(2,128)}, u32[]{:S(2)}) copy-start(s32[128,2]{0,1:T(2,128)} %param.9) | copy-start | bytes 3076
  137.3 11.6 %copy-start.2 = (f32[8]{0:T(128)S(1)}, f32[8]{0:T(128)}, u32[]{:S(2)}) copy-start(f32[8]{0:T(128)} %param.8) | copy-start | bytes 100
  145.2 17.9 %all-to-all-start = ((f32[512,2,144]{2,1,0:T(2,128)}), f32[512,2,144]{2,1,0:T(2,128)S(1)}, u32[]{:S(2)}, u32[]{:S(2)}) async-start(f32[512,2,144]{2,1,0:T(2,128)} %copy.24), calls=%async_computation | async-start | bytes 2097152 | tf_op jit(solution)/shard_map/all_to_all | solution.py:46
  148.8 180.1 %reduce-scatter.2.cloned.1.call-start = ((), (), s32[]{:S(2)}) async-start(), calls=%async_computation.5 | async-start | bytes 9289728 | tf_op jit(solution)/shard_map/reduce_scatter | solution.py:51
  165.0 17.5 %copy-start.1 = (f32[128]{0:T(128)}, f32[128]{0:T(128)S(1)}, u32[]{:S(2)}) copy-start(f32[128]{0:T(128)S(1)} %log_add_fusion) | copy-start | bytes 1540
Sparse Core Ops, SparseCore 0:
  10.1 74.7 all-gather.4
  86.4 50.8 all-gather.2
  182.6 146.1 reduce-scatter.1
where the time goes:
time: 336 us; the launch traced here: 335 us
  waiting for transfers between devices  264 us (79%)
  blocking collectives  31.3 us (9%)
  matrix products  15.2 us (5%)
  between operations  13.8 us (4%)
  other arithmetic  4.49 us (1%)
  starting transfers between devices  3.63 us (1%)
    reduce_scatter x1, waiting for transfers between devices, local(): class_sums = lax.psum_scatter(sums, 'prt', scatter_dimension=2, tiled=True)  124 us
    all_gather x1, waiting for transfers between devices, score_columns(): piece = lax.all_gather(slab, 'prt', axis=2, tiled=True)  76.2 us
    all_gather x1, waiting for transfers between devices, local(): everyone = lax.all_gather(images, 'cls', axis=0, tiled=True)  49 us
    psum x1, blocking collectives, local(): class_weights = lax.psum(totals, 'prt')  22.6 us
    all_to_all x1, waiting for transfers between devices, local(): lax.all_to_all(own_scores, 'cls', split_axis=0, concat_axis=1, tiled=True)  14.1 us
    all_to_all x1, blocking collectives, local(): mine = lax.all_to_all(post, 'cls', split_axis=1, concat_axis=0, tiled=True)  8.72 us
    dot_general x1, matrix products, local(): jnp.einsum('ijr,if->jrf', mine, everyone, preferred_element_type=jnp.floa...  8.56 us
  transfers between devices with their start and end apart: 4, of which 4 were waited for; matrix products, arithmetic and copies ran while one was open for 1% of the time, Pallas kernels for 0%

commit v1 on v0

--- a/solution.py
+++ b/solution.py
@@ -4,11 +4,35 @@
 from jax.sharding import PartitionSpec as P
 
 
+def local_data_update(local_x, at_axis):
+    local_x = jnp.moveaxis(local_x, 0, at_axis)
+    prior = local_x.shape
+    return local_x.reshape(
+        *prior[:at_axis], prior[at_axis] * prior[at_axis + 1], *prior[at_axis + 2 :]
+    )
+
+
 def score_columns(slab, weighted, noise_weights):
     count = slab.shape[0]
     orient = slab.shape[1]
     nrows = weighted.shape[0]
-    piece = lax.all_gather(slab, "prt", axis=2, tiled=True)
+    slots = lax.axis_size("prt")
+    lanes = tuple(((dev, (dev + 1) % slots) for dev in range(slots)))
+    pile = tuple(((nth, dd) for dd, nth in lanes))
+    y_new, z = ([], [])
+    for kk in range(slots - 1):
+        if kk % 2 == 0:
+            u_next = lax.ppermute(y_new[-1] if y_new else slab, axis_name="prt", perm=lanes)
+            y_new.append(u_next)
+        else:
+            vec_out = lax.ppermute(z[-1] if z else slab, axis_name="prt", perm=pile)
+            z.append(vec_out)
+    moved = jnp.stack([*y_new[::-1], slab, *z], 0)
+    parts_out = lax.axis_index("prt")
+    taken_in = len(y_new)
+    near = parts_out - taken_in
+    moved = moved[(jnp.arange(slots) - near) % slots]
+    piece = local_data_update(moved, 2)
     span = piece.shape[2]
     flat = piece.reshape(count * orient, span)
     cross = lax.dot_general(

time: 336 us -> 313 us (0.932)
  waiting for transfers between devices: 264 us -> 187 us
  starting transfers between devices: 3.63 us -> 41.1 us
  local copies, waits for them, and re-layouts: 2.64 us -> 22.9 us
    all_gather x1 -> x0, waiting for transfers between devices: 76.2 us -> none  [score_columns(): piece = lax.all_gather(slab, 'prt', axis=2, tiled=True)]
    all_gather x1, waiting for transfers between devices: 49 us -> 0.01 us  [local(): everyone = lax.all_gather(images, 'cls', axis=0, tiled=True)]
    ppermute x0 -> x7, waiting for transfers between devices: none -> 48.7 us  [the longest x4 48.7 us: score_columns(): lax.ppermute(y_new[-1] if y_new else slab, axis_name='prt', perm=lanes)]
    ppermute x0 -> x7, starting transfers between devices: none -> 37.5 us  [the longest x3 29.5 us: score_columns(): vec_out = lax.ppermute(z[-1] if z else slab, axis_name='prt', perm=pile)]
    unnamed x6 -> x20, local copies, waits for them, and re-layouts: 0.01 us -> 10 us
    gather x0 -> x1, local copies, waits for them, and re-layouts: none -> 5.12 us  [score_columns(): moved = moved[(jnp.arange(slots) - near) % slots]]
    transpose x0 -> x1, local copies, waits for them, and re-layouts: none -> 3.55 us  [local_data_update(): local_x = jnp.moveaxis(local_x, 0, at_axis)]
  transfers between devices with their start and end apart: 4 -> 10, of which waited for: 4 -> 6; matrix products, arithmetic and copies ran while one was open for 1% -> 7% of each run, Pallas kernels for 0% -> 0%
where the time goes in v1:
time: 313 us; the launch traced here: 312 us
  waiting for transfers between devices  187 us (60%)
  starting transfers between devices  41.1 us (13%)
  blocking collectives  29.8 us (10%)
  local copies, waits for them, and re-layouts  22.9 us (7%)
  matrix products  15.2 us (5%)
  between operations  14.2 us (5%)
    reduce_scatter x1, waiting for transfers between devices, local(): class_sums = lax.psum_scatter(sums, 'prt', scatter_dimension=2, tiled=True)  123 us
    ppermute x4, waiting for transfers between devices, score_columns(): lax.ppermute(y_new[-1] if y_new else slab, axis_name='prt', perm=lanes)  48.7 us
    ppermute x3, starting transfers between devices, score_columns(): vec_out = lax.ppermute(z[-1] if z else slab, axis_name='prt', perm=pile)  29.5 us
    psum x1, blocking collectives, local(): class_weights = lax.psum(totals, 'prt')  21 us
    all_to_all x1, waiting for transfers between devices, local(): lax.all_to_all(own_scores, 'cls', split_axis=0, concat_axis=1, tiled=True)  14.1 us
    unnamed x20, local copies, waits for them, and re-layouts  10 us
    all_to_all x1, blocking collectives, local(): mine = lax.all_to_all(post, 'cls', split_axis=1, concat_axis=0, tiled=True)  8.72 us
    dot_general x1, matrix products, local(): jnp.einsum('ijr,if->jrf', mine, everyone, preferred_element_type=jnp.floa...  8.56 us
  transfers between devices with their start and end apart: 10, of which 6 were waited for; matrix products, arithmetic and copies ran while one was open for 7% of the time, Pallas kernels for 0%

profile of v1, /device:TPU:0, one launch (start us, length us, event | category | flops | bytes accessed | tf_op | source)
XLA Modules:
  0.0 312.2 jit_solution(13175010031791548189)
XLA Ops:
  7.9 3.0 collective-permute-start
  11.0 15.0 %collective-permute-done = bf16[2,144,896]{2,1,0:T(8,128)(2,1)S(1)} collective-permute-done((bf16[2,144,896]{2,1,0:T(8,128)(2,1)}, bf16[2,144,896]{2,1,0:T(8,128)(2,1)S(1)}, u32[]{:S(2)}, u32[]{:S(2)}) %collective-permute-start) | collective-permute-done | bytes 516128 | tf_op jit(solution)/shard_map/ppermute | solution.py:25
  26.0 4.7 %collective-permute-start.4 = (bf16[2,144,896]{2,1,0:T(8,128)(2,1)}, bf16[2,144,896]{2,1,0:T(8,128)(2,1)S(1)}, u32[]{:S(2)}, u32[]{:S(2)}) collective-permute-start(bf16[2,144,896]{2,1,0:T(8,128)(2,1)} %param.6), channel_id=1, source_target_pairs={{1,0},{2,1},{3,2},{4,3},{5,4},{6,5},{7,6},{0,7},{9,8},{10,9},{11,1... | collective-permute-start | bytes 1548296 | tf_op jit(solution)/shard_map/ppermute | solution.py:28
  30.7 17.1 %collective-permute-done.1 = bf16[2,144,896]{2,1,0:T(8,128)(2,1)S(1)} collective-permute-done((bf16[2,144,896]{2,1,0:T(8,128)(2,1)S(1)}, bf16[2,144,896]{2,1,0:T(8,128)(2,1)S(1)}, u32[]{:S(2)}, u32[]{:S(2)}) %collective-permute-start.1) | collective-permute-done | bytes 516128 | tf_op jit(solution)/shard_map/ppermute | solution.py:25
  47.7 2.5 collective-permute-start.2
  50.2 12.2 %collective-permute-start.5 = (bf16[2,144,896]{2,1,0:T(8,128)(2,1)S(1)}, bf16[2,144,896]{2,1,0:T(8,128)(2,1)S(1)}, u32[]{:S(2)}, u32[]{:S(2)}) collective-permute-start(bf16[2,144,896]{2,1,0:T(8,128)(2,1)S(1)} %collective-permute-done.4), channel_id=1, source_target_pairs={{1,0},{2,1},{3,2},{4,3},{5,4},{6,5},{7,6},{0,7},{9,8},{10,9},{11,1... | collective-permute-start | bytes 1548296 | tf_op jit(solution)/shard_map/ppermute | solution.py:28
  62.4 8.9 %collective-permute-done.2 = bf16[2,144,896]{2,1,0:T(8,128)(2,1)S(1)} collective-permute-done((bf16[2,144,896]{2,1,0:T(8,128)(2,1)S(1)}, bf16[2,144,896]{2,1,0:T(8,128)(2,1)S(1)}, u32[]{:S(2)}, u32[]{:S(2)}) %collective-permute-start.2) | collective-permute-done | bytes 516128 | tf_op jit(solution)/shard_map/ppermute | solution.py:25
  71.2 2.5 collective-permute-start.3
  74.5 12.6 %collective-permute-start.6 = (bf16[2,144,896]{2,1,0:T(8,128)(2,1)S(1)}, bf16[2,144,896]{2,1,0:T(8,128)(2,1)S(1)}, u32[]{:S(2)}, u32[]{:S(2)}) collective-permute-start(bf16[2,144,896]{2,1,0:T(8,128)(2,1)S(1)} %collective-permute-done.5), channel_id=1, source_target_pairs={{1,0},{2,1},{3,2},{4,3},{5,4},{6,5},{7,6},{0,7},{9,8},{10,9},{11,1... | collective-permute-start | bytes 1548296 | tf_op jit(solution)/shard_map/ppermute | solution.py:28
  87.1 7.8 %collective-permute-done.3 = bf16[2,144,896]{2,1,0:T(8,128)(2,1)} collective-permute-done((bf16[2,144,896]{2,1,0:T(8,128)(2,1)S(1)}, bf16[2,144,896]{2,1,0:T(8,128)(2,1)}, u32[]{:S(2)}, u32[]{:S(2)}) %collective-permute-start.3) | collective-permute-done | bytes 516128 | tf_op jit(solution)/shard_map/ppermute | solution.py:25
  94.9 1.9 bitcast_dynamic-update-slice_fusion.7
  102.7 5.1 %gather_fusion = bf16[8,2,144,896]{3,2,1,0:T(8,128)(2,1)} fusion(bf16[8,2,144,896]{3,2,1,0:T(8,128)(2,1)} %bitcast_dynamic-update-slice_fusion, s32[1024]{0:T(1024)S(1)} %pad_clamp_fusion), kind=kCustom, calls=%fused_computation | custom fusion | bytes 8257568 | tf_op jit(solution)/shard_map/gather | solution.py:34
  107.8 3.5 %copy.27 = bf16[2,144,8,896]{3,2,1,0:T(8,128)(2,1)S(1)} copy(bf16[2,144,8,896]{3,1,0,2:T(8,128)(2,1)} %bitcast.51) | data formatting | bytes 8257536 | tf_op jit(solution)/shard_map/transpose | solution.py:8
  111.4 2.8 copy.36
  114.5 1.2 multiply_reduce_fusion
  115.8 6.6 %fusion.4 = f32[512,288]{0,1:T(8,128)S(1)} fusion(bf16[288,7168]{1,0:T(8,128)(2,1)} %bitcast.55, bf16[512,7168]{1,0:T(8,128)(2,1)} %all-gather.2.cloned.1.call-done, f32[7168]{0:T(1024)S(1)} %copy-done.2, f32[288]{0:T(512)S(1)} %mul.44), kind=kOutput, calls=%fused_computation.7 | convolution fusion | flops 2125086720 | bytes 12088448 | tf_op jit(solution)/shard_map/dot_general | solution.py:38
  122.4 1.3 copy.28
  123.7 3.5 %all-to-all-start = ((f32[512,2,144]{2,1,0:T(2,128)}), f32[512,2,144]{2,1,0:T(2,128)S(1)}, u32[]{:S(2)}, u32[]{:S(2)}) async-start(f32[512,2,144]{2,1,0:T(2,128)} %copy.28), calls=%async_computation | async-start | bytes 2097152 | tf_op jit(solution)/shard_map/all_to_all | solution.py:70
  127.5 14.1 %all-to-all-done = f32[512,2,144]{2,1,0:T(2,128)S(1)} async-done(((f32[512,2,144]{2,1,0:T(2,128)}), f32[512,2,144]{2,1,0:T(2,128)S(1)}, u32[]{:S(2)}, u32[]{:S(2)}) %all-to-all-start) | async-done | bytes 589856 | tf_op jit(solution)/shard_map/all_to_all | solution.py:70
  141.6 1.0 copy.34
  143.7 8.7 %all_to_all.36 = bf16[128,8,144]{0,2,1:T(8,128)(2,1)S(1)} all-to-all(bf16[128,8,144]{0,2,1:T(8,128)(2,1)S(1)} %fusion.8), channel_id=1, replica_groups=mesh['cls'=4,'prt'=8] {'cls'}, dimensions={1} | all-to-all | bytes 589824 | tf_op jit(solution)/shard_map/all_to_all | solution.py:72
  152.4 8.6 %fusion.1 = f32[2,144,7168]{2,1,0:T(8,128)} fusion(bf16[512,7168]{1,0:T(8,128)(2,1)} %all-gather.2.cloned.1.call-done, bf16[4,2,18,8,128]{4,3,2,1,0:T(8,128)(2,1)S(1)} %bitcast.56), kind=kOutput, calls=%fused_computation.4 | convolution fusion | flops 2113929216 | bytes 15892480 | tf_op jit(solution)/shard_map/ijr,if->jrf/dot_general | solution.py:73
  161.1 21.0 %psum.7 = f32[2,144]{1,0:T(2,128)} all-reduce(f32[2,144]{1,0:T(2,128)S(1)} %convert_reduce_fusion), channel_id=1, replica_groups=mesh['cls'=4,'prt'=8] {'prt'}, use_global_device_ids=true, to_apply=%region_6.7 | all-reduce | flops 288 | bytes 2304 | tf_op jit(solution)/shard_map/psum | solution.py:76
  182.2 123.2 %reduce-scatter.2.cloned.1.call-done = f32[2,144,896]{2,1,0:T(8,128)} async-done(((f32[2,144,7168]{2,1,0:T(8,128)}), f32[2,144,896]{2,1,0:T(8,128)}) %reduce-scatter.2.cloned.1.call-update) | async-done | bytes 1032208 | tf_op jit(solution)/shard_map/reduce_scatter | solution.py:75
  (45 shorter events, 9.3 us)
Async XLA Ops:
  7.2 92.2 %copy-start.1 = (bf16[2,144,896]{2,1,0:T(8,128)(2,1)S(1)}, bf16[2,144,896]{2,1,0:T(8,128)(2,1)}, u32[]{:S(2)}) copy-start(bf16[2,144,896]{2,1,0:T(8,128)(2,1)} %param.6) | copy-start | bytes 1548292
  7.2 108.6 %all-gather.2.cloned.1.call-start = ((), (), s32[]{:S(2)}) async-start(), calls=%async_computation.3 | async-start | bytes 9175040 | tf_op jit(solution)/shard_map/all_gather | solution.py:67
  7.9 18.0 %collective-permute-start = (bf16[2,144,896]{2,1,0:T(8,128)(2,1)}, bf16[2,144,896]{2,1,0:T(8,128)(2,1)S(1)}, u32[]{:S(2)}, u32[]{:S(2)}) collective-permute-start(bf16[2,144,896]{2,1,0:T(8,128)(2,1)} %param.6), channel_id=1, source_target_pairs={{0,1},{1,2},{2,3},{3,4},{4,5},{5,6},{6,7},{7,0},{8,9},{9,10},{10,1... | collective-permute-start | bytes 1548296 | tf_op jit(solution)/shard_map/ppermute | solution.py:25
  26.0 21.8 %collective-permute-start.1 = (bf16[2,144,896]{2,1,0:T(8,128)(2,1)S(1)}, bf16[2,144,896]{2,1,0:T(8,128)(2,1)S(1)}, u32[]{:S(2)}, u32[]{:S(2)}) collective-permute-start(bf16[2,144,896]{2,1,0:T(8,128)(2,1)S(1)} %collective-permute-done), channel_id=1, source_target_pairs={{0,1},{1,2},{2,3},{3,4},{4,5},{5,6},{6,7},{7,0},{8,9},{9,10},{10,1... | collective-permute-start | bytes 1548296 | tf_op jit(solution)/shard_map/ppermute | solution.py:25
  26.0 24.3 %collective-permute-start.4 = (bf16[2,144,896]{2,1,0:T(8,128)(2,1)}, bf16[2,144,896]{2,1,0:T(8,128)(2,1)S(1)}, u32[]{:S(2)}, u32[]{:S(2)}) collective-permute-start(bf16[2,144,896]{2,1,0:T(8,128)(2,1)} %param.6), channel_id=1, source_target_pairs={{1,0},{2,1},{3,2},{4,3},{5,4},{6,5},{7,6},{0,7},{9,8},{10,9},{11,1... | collective-permute-start | bytes 1548296 | tf_op jit(solution)/shard_map/ppermute | solution.py:28
  47.7 23.5 %collective-permute-start.2 = (bf16[2,144,896]{2,1,0:T(8,128)(2,1)S(1)}, bf16[2,144,896]{2,1,0:T(8,128)(2,1)S(1)}, u32[]{:S(2)}, u32[]{:S(2)}) collective-permute-start(bf16[2,144,896]{2,1,0:T(8,128)(2,1)S(1)} %collective-permute-done.1), channel_id=1, source_target_pairs={{0,1},{1,2},{2,3},{3,4},{4,5},{5,6},{6,7},{7,0},{8,9},{9,10},{10,1... | collective-permute-start | bytes 1548296 | tf_op jit(solution)/shard_map/ppermute | solution.py:25
  50.2 24.3 %collective-permute-start.5 = (bf16[2,144,896]{2,1,0:T(8,128)(2,1)S(1)}, bf16[2,144,896]{2,1,0:T(8,128)(2,1)S(1)}, u32[]{:S(2)}, u32[]{:S(2)}) collective-permute-start(bf16[2,144,896]{2,1,0:T(8,128)(2,1)S(1)} %collective-permute-done.4), channel_id=1, source_target_pairs={{1,0},{2,1},{3,2},{4,3},{5,4},{6,5},{7,6},{0,7},{9,8},{10,9},{11,1... | collective-permute-start | bytes 1548296 | tf_op jit(solution)/shard_map/ppermute | solution.py:28
  71.2 23.7 %collective-permute-start.3 = (bf16[2,144,896]{2,1,0:T(8,128)(2,1)S(1)}, bf16[2,144,896]{2,1,0:T(8,128)(2,1)}, u32[]{:S(2)}, u32[]{:S(2)}) collective-permute-start(bf16[2,144,896]{2,1,0:T(8,128)(2,1)S(1)} %collective-permute-done.2), channel_id=1, source_target_pairs={{0,1},{1,2},{2,3},{3,4},{4,5},{5,6},{6,7},{7,0},{8,9},{9,10},{10,1... | collective-permute-start | bytes 1548296 | tf_op jit(solution)/shard_map/ppermute | solution.py:25
  74.5 27.4 %collective-permute-start.6 = (bf16[2,144,896]{2,1,0:T(8,128)(2,1)S(1)}, bf16[2,144,896]{2,1,0:T(8,128)(2,1)S(1)}, u32[]{:S(2)}, u32[]{:S(2)}) collective-permute-start(bf16[2,144,896]{2,1,0:T(8,128)(2,1)S(1)} %collective-permute-done.5), channel_id=1, source_target_pairs={{1,0},{2,1},{3,2},{4,3},{5,4},{6,5},{7,6},{0,7},{9,8},{10,9},{11,1... | collective-permute-start | bytes 1548296 | tf_op jit(solution)/shard_map/ppermute | solution.py:28
  111.4 3.1 copy-start
  114.5 1.3 copy-start.2
  115.8 11.5 %copy-start.3 = (s32[128,2]{0,1:T(2,128)S(1)}, s32[128,2]{0,1:T(2,128)}, u32[]{:S(2)}) copy-start(s32[128,2]{0,1:T(2,128)} %param.9) | copy-start | bytes 3076
  115.8 11.5 %copy-start.5 = (f32[8]{0:T(128)S(1)}, f32[8]{0:T(128)}, u32[]{:S(2)}) copy-start(f32[8]{0:T(128)} %param.8) | copy-start | bytes 100
  123.7 17.9 %all-to-all-start = ((f32[512,2,144]{2,1,0:T(2,128)}), f32[512,2,144]{2,1,0:T(2,128)S(1)}, u32[]{:S(2)}, u32[]{:S(2)}) async-start(f32[512,2,144]{2,1,0:T(2,128)} %copy.28), calls=%async_computation | async-start | bytes 2097152 | tf_op jit(solution)/shard_map/all_to_all | solution.py:70
  127.2 178.1 %reduce-scatter.2.cloned.1.call-start = ((), (), s32[]{:S(2)}) async-start(), calls=%async_computation.4 | async-start | bytes 9289728 | tf_op jit(solution)/shard_map/reduce_scatter | solution.py:75
  143.4 17.5 %copy-start.4 = (f32[128]{0:T(128)}, f32[128]{0:T(128)S(1)}, u32[]{:S(2)}) copy-start(f32[128]{0:T(128)S(1)} %log_add_fusion) | copy-start | bytes 1540
Sparse Core Ops, SparseCore 0:
  9.5 55.0 all-gather.1
  161.1 144.1 reduce-scatter.1
